TPU v7x, 128 devices: a whole 4x4x4 slice. The times are simulated.
128 devices in a mesh: rows: 32 (over z, y, core), aux: 4 (over x).
Axes of the slice: x: 4, y: 4, z: 4, core: 2. Of those that a mesh axis runs over, the one named last changes fastest.
Arguments:
- density: bfloat16 [128, 8, 16384], P('aux', None, 'rows'), may hold values from -64 to 64, as said below
- vir_coeffs: bfloat16 [16384, 16384], P('rows'), may hold values from -0.046875 to 0.046875
- occ_coeffs: bfloat16 [8, 16384], P(None, 'rows'), may hold values from -2 to 2
- shell_len: int32 [32, 64], replicated, may hold values from 1 to 16, 512 in all within a row
- mu_shell: int32 [8192], P('rows'), may hold values from 0 to 2047
- nu_shell: int32 [8192], P('rows'), may hold values from 0 to 63
- owner: int32 [8192, 1], P('rows'), may hold values from 0 to 31; in each aligned block of 256 rows (0 to 255, 256 to 511, ...) at most 16 rows name the same one
Outputs:
- pair_blocks: bfloat16 [16384, 128, 256], P('rows', 'aux')
- pair_scale: float32 [16384], P('rows')
Inputs may be any that keep to these rules, and one draw needn't show every extreme that they name: Each index of rows names at most 16 of its 256 pairs for one owner, and exactly 16 for some owner. `shell_len`: shell lengths of each slab sum to 512; the longest is 16. `density`: Real-valued, of varying scale over auxiliary functions and orbital pairs.
All inputs are finite; a program needn't handle non-finite values.
Results may differ from a plain program's by a relative error of at most 0.0049.
Values may be sent and summed in bfloat16 or wider, within the bound.
A program may use at most 192 MiB of HBM per device.

v0:
```python
import jax
import jax.numpy as jnp
from jax import lax
from jax.sharding import PartitionSpec as P

NAUX = 128
PAD = 16


def lookup(table, index):
    hits = index[:, None] == jnp.arange(table.shape[0], dtype=jnp.int32)[None, :]
    return jnp.sum(jnp.where(hits, table[None, :], 0), axis=1)


def per_device(density, vir_coeffs, occ_coeffs, shell_len, mu_shell, nu_shell, owner):
    row_count = lax.axis_size("rows")
    position = lax.axis_index("rows")
    slab = vir_coeffs.shape[0]
    local_aux = density.shape[0]
    occupied = density.shape[1]
    pair_count = mu_shell.shape[0]
    capacity = 2 * pair_count // row_count
    slot_total = row_count * capacity
    half = jnp.einsum(
        "pia,na->pin",
        lax.all_gather(density, "rows", axis=2, tiled=True),
        vir_coeffs,
        preferred_element_type=jnp.float32,
    ).astype(jnp.bfloat16)
    occ_full = lax.all_gather(occ_coeffs, "rows", axis=1, tiled=True)
    starts = jnp.cumsum(shell_len, axis=1) - shell_len
    flat_start = (starts + jnp.arange(row_count, dtype=jnp.int32)[:, None] * slab).reshape(-1)
    flat_len = shell_len.reshape(-1)
    mu_start = lookup(flat_start, mu_shell)
    mu_length = lookup(flat_len, mu_shell)
    own_start = lax.dynamic_index_in_dim(starts, position, 0, keepdims=False)
    own_length = lax.dynamic_index_in_dim(shell_len, position, 0, keepdims=False)
    nu_start = lookup(own_start, nu_shell)
    nu_length = lookup(own_length, nu_shell)
    target = owner[:, 0]
    onehot = (target[:, None] == jnp.arange(row_count, dtype=jnp.int32)[None, :]).astype(jnp.int32)
    earlier = jnp.cumsum(onehot, axis=0) - onehot
    rank = jnp.sum(earlier * onehot, axis=1)
    send_row = target * capacity + rank
    placed = send_row[None, :] == jnp.arange(slot_total, dtype=jnp.int32)[:, None]
    live = jnp.any(placed, axis=1)
    slot_mu_start = jnp.sum(jnp.where(placed, mu_start[None, :], 0), axis=1)
    slot_mu_length = jnp.sum(jnp.where(placed, mu_length[None, :], 0), axis=1)
    slot_nu_start = jnp.sum(jnp.where(placed, nu_start[None, :], 0), axis=1)
    slot_nu_length = jnp.sum(jnp.where(placed, nu_length[None, :], 0), axis=1)
    offsets = jnp.arange(PAD, dtype=jnp.int32)
    nu_column = (slot_nu_start[:, None] + offsets[None, :]).reshape(-1)
    nu_valid = ((offsets[None, :] < slot_nu_length[:, None]) & live[:, None]).reshape(-1)
    selector = (
        (nu_column[:, None] == jnp.arange(slab, dtype=jnp.int32)[None, :]) & nu_valid[:, None]
    ).astype(jnp.bfloat16)
    half_slots = jnp.einsum(
        "pin,xn->pix", half, selector, preferred_element_type=jnp.float32
    ).astype(jnp.bfloat16)
    mu_column = (slot_mu_start[:, None] + offsets[None, :]).reshape(-1)
    mu_valid = ((offsets[None, :] < slot_mu_length[:, None]) & live[:, None]).reshape(-1)
    occ_pad = jnp.pad(occ_full, ((0, 0), (0, PAD)))
    coeff_slots = jnp.where(
        mu_valid[None, :], jnp.take(occ_pad, mu_column, axis=1), jnp.zeros((), jnp.bfloat16)
    )
    blocks = jnp.einsum(
        "ism,pisn->spmn",
        coeff_slots.reshape(occupied, slot_total, PAD),
        half_slots.reshape(local_aux, occupied, slot_total, PAD),
        preferred_element_type=jnp.float32,
    )
    outgoing = blocks.astype(jnp.bfloat16).reshape(slot_total, local_aux, PAD * PAD)
    received = lax.all_to_all(outgoing, "rows", split_axis=0, concat_axis=0, tiled=True)
    partial_squares = jnp.sum(jnp.square(received.astype(jnp.float32)), axis=(1, 2))
    total = lax.psum(partial_squares, "aux")
    pair_scale = jnp.sqrt(total / (NAUX * PAD * PAD) + 1e-06)
    return (received, pair_scale)


def solution(mesh):
    return jax.shard_map(
        per_device,
        mesh=mesh,
        in_specs=(
            P("aux", None, "rows"),
            P("rows", None),
            P(None, "rows"),
            P(),
            P("rows"),
            P("rows"),
            P("rows", None),
        ),
        out_specs=(P("rows", "aux", None), P("rows")),
        check_vma=False,
    )
```

profile of v0, /device:TPU:24, one launch (start us, length us, event | category | flops | bytes accessed | tf_op | source)
XLA Modules:
  0.0 325.7 jit_solution(17420208919459613433)
XLA Ops:
  7.9 0.8 broadcast_in_dim.133
  8.7 0.9 reduce_window_sum.28
  9.6 0.8 broadcast_add_fusion
  10.5 0.7 fusion.27
  12.0 0.7 dynamic-slice_bitcast_fusion
  12.7 0.8 fusion.26
  13.5 0.8 select_reduce_fusion.6
  14.2 1.4 select_reduce_fusion.1
  17.6 0.9 copy.36
  19.0 30.7 %all_gather.7 = bf16[8,16384]{0,1:T(8,128)(2,1)S(1)} all-gather(bf16[8,512]{0,1:T(8,128)(2,1)S(1)} %copy.36), channel_id=1, replica_groups=mesh['rows'=32,'aux'=4] {'rows'}, dimensions={1}, use_global_device_ids=true | all-gather | bytes 270336 | tf_op jit(solution)/shard_map/all_gather | solution.py:30
  49.7 2.7 pad.4
  52.5 24.6 %gather_fusion = bf16[8192,8]{1,0:T(8,128)(2,1)S(1)} fusion(bf16[8,16400]{0,1:T(8,128)(2,1)} %pad.4, s32[8192]{0:T(1024)S(1)} %broadcast_clamp_fusion), kind=kCustom, calls=%fused_computation | custom fusion | bytes 294912 | tf_op jit(solution)/shard_map/jit(_take)/gather | solution.py:64
  77.1 1.0 copy.38
  78.2 10.7 %fusion.11 = bf16[32,8,512]{2,1,0:T(8,128)(2,1)S(1)} fusion(bf16[32,8,16384]{2,1,0:T(8,128)(2,1)} %all-gather.2.cloned.1.call-done, bf16[512,16384]{1,0:T(8,128)(2,1)} %param.8), kind=kOutput, calls=%fused_computation.15 | convolution fusion | flops 4295098368 | bytes 25427968 | tf_op jit(solution)/shard_map/pia,na->pin/dot_general | solution.py:24
  88.9 6.9 %fusion.6 = bf16[32,8,8192]{2,1,0:T(8,128)(2,1)} fusion(bf16[32,8,512]{2,1,0:T(8,128)(2,1)S(1)} %fusion.11, s32[8192]{0:T(1024)S(1)} %add.108, pred[8192]{0:T(1024)(128)(4,1)S(1)} %and.44), kind=kOutput, calls=%fused_computation.9 | convolution fusion | flops 2157969408 | bytes 4497408 | tf_op jit(solution)/shard_map/pin,xn->pix/dot_general | solution.py:57
  95.8 17.7 %copy.43 = bf16[32,8,8192]{0,1,2:T(8,128)(2,1)} copy(bf16[32,8,8192]{2,1,0:T(8,128)(2,1)} %fusion.6) | data formatting | bytes 8388608 | tf_op jit(solution)/shard_map/reshape | solution.py:69
  113.5 19.8 %convert_bitcast_fusion = bf16[512,32,16,16]{1,2,3,0:T(8,128)(2,1)} fusion(bf16[32,8,512,16]{0,1,3,2:T(8,128)(2,1)} %bitcast.52, bf16[8,512,16]{2,0,1:T(8,128)(2,1)S(1)} %copy.38, pred[512,16]{1,0:T(8,128)(4,1)S(1)} %copy.35, pred[512,16]{1,0:T(8,128)(4,1)S(1)} %get-tuple-element.14), kind=kOutput, calls=%fused_computation.1 | convolution fusion | flops 71434240 | bytes 12730368 | tf_op jit(solution)/shard_map/ism,pisn->spmn/dot_general | solution.py:66
  133.2 48.5 %copy.40 = bf16[512,32,16,16]{0,3,2,1:T(8,128)(2,1)} copy(bf16[512,32,16,16]{1,2,3,0:T(8,128)(2,1)} %convert_bitcast_fusion) | data formatting | bytes 16777216 | tf_op jit(solution)/shard_map/convert_element_type | solution.py:72
  181.8 14.7 %copy.41 = bf16[512,32,256]{2,1,0:T(8,128)(2,1)} copy(bf16[512,32,256]{0,2,1:T(8,128)(2,1)} %bitcast.53) | data formatting | bytes 16777216 | tf_op jit(solution)/shard_map/reshape | solution.py:72
  196.4 98.1 %all_to_all.5 = bf16[512,32,256]{2,1,0:T(8,128)(2,1)S(1)} all-to-all(bf16[512,32,256]{2,1,0:T(8,128)(2,1)} %copy.41), channel_id=1, replica_groups=mesh['rows'=32,'aux'=4] {'rows'}, dimensions={0} | all-to-all | bytes 16777216 | tf_op jit(solution)/shard_map/all_to_all | solution.py:73
  294.6 3.2 copy-done
  297.8 2.2 multiply_reduce_fusion
  300.0 10.5 %psum.7 = f32[512]{0:T(512)S(1)} all-reduce(f32[512]{0:T(512)S(1)} %multiply_reduce_fusion), channel_id=1, replica_groups=mesh['rows'=32,'aux'=4] {'aux'}, use_global_device_ids=true, to_apply=%region_14.15 | all-reduce | flops 512 | bytes 4096 | tf_op jit(solution)/shard_map/psum | solution.py:75
  311.1 7.8 %copy.47 = bf16[512,32,256]{2,1,0:T(8,128)(2,1)} copy(bf16[512,32,256]{2,1,0:T(8,128)(2,1)} %copy-done) | data formatting | bytes 16777216
  (25 shorter events, 4.6 us)
Async XLA Ops:
  7.2 71.0 %all-gather.2.cloned.1.call-start = ((), (), s32[]{:S(2)}) async-start(), calls=%async_computation.1 | async-start | bytes 8650752 | tf_op jit(solution)/shard_map/all_gather | solution.py:26
  294.6 3.2 copy-start
Sparse Core Ops, SparseCore 0:
  10.2 61.9 all-gather.1
where the time goes:
time: 330 us; the launch traced here: 326 us
  blocking collectives  139 us (42%)
  local copies, waits for them, and re-layouts  124 us (38%)
  matrix products  37.4 us (11%)
  between operations  14.2 us (4%)
  other arithmetic  10.5 us (3%)
    all_to_all x1, blocking collectives, per_device(): lax.all_to_all(outgoing, 'rows', split_axis=0, concat_axis=0, tiled=True)  98.1 us
    convert_element_type x1, local copies, waits for them, and re-layouts, per_device(): blocks.astype(jnp.bfloat16).reshape(slot_total, local_aux, PAD * PAD)  48.5 us
    all_gather x1, blocking collectives, per_device(): occ_full = lax.all_gather(occ_coeffs, 'rows', axis=1, tiled=True)  30.7 us
    gather x2, local copies, waits for them, and re-layouts, per_device(): jnp.take(occ_pad, mu_column, axis=1)  25.6 us
    dot_general x1, matrix products, per_device(): jnp.einsum('ism,pisn->spmn', coeff_slots.reshape(occupied, slot_total, PA...  19.8 us
    reshape x1, local copies, waits for them, and re-layouts, per_device(): half_slots.reshape(local_aux, occupied, slot_total, PAD)  17.7 us
    reshape x1, local copies, waits for them, and re-layouts, per_device(): blocks.astype(jnp.bfloat16).reshape(slot_total, local_aux, PAD * PAD)  14.7 us
    unnamed x4, local copies, waits for them, and re-layouts  11.8 us
  transfers between devices with their start and end apart: 1, of which 0 were waited for; matrix products, arithmetic and copies ran while one was open for 12% of the time, Pallas kernels for 0%

commit v1 on v0

v1 whole, which is shorter than its diff:
```python
import jax
import jax.numpy as jnp
from jax import lax
from jax.experimental import pallas as pl
from jax.experimental.pallas import tpu as pltpu
from jax.sharding import PartitionSpec as P

NY = 4
NZ = 4
NCHIP = NY * NZ
NROW = 2 * NCHIP
NX = 4
UNITS = 4
OCC = 8
PAD = 16
CAP = 16
F32 = jnp.float32
BF16 = jnp.bfloat16
I32 = jnp.int32
ORDER = [(0, 0), (1, 0), (0, 1), (3, 0), (0, 3), (2, 0), (0, 2), (1, 1), (3, 3), (1, 3), (3, 1),
         (2, 1), (1, 2), (2, 3), (3, 2), (2, 2)]


def pick(t, values):
    out = jnp.int32(values[0])
    for k in range(1, len(values)):
        out = jnp.where(t == k, jnp.int32(values[k]), out)
    return out


def iota(shape, dim):
    return lax.broadcasted_iota(I32, shape, dim)


def dot(a, b):
    return lax.dot_general(a, b, (((1,), (0,)), ((), ())), preferred_element_type=F32)


def dot_nt(a, b):
    return lax.dot_general(a, b, (((1,), (1,)), ((), ())), preferred_element_type=F32)


def kernel(dens, vir, extra, slen, out, total_out,
           dg, hg, cbuf, eg, acc, occf, spread, rolled, cexp, squares, sumbuf, sumout, vtab,
           stab, ptab,
           dens_sem, vir_sem, d_recv, h_recv, d_send, h_send, e_send, x_recv, x_send, t_sem):
    row = lax.axis_index("rows")
    ax = lax.axis_index("aux")
    core = lax.rem(row, 2)
    y = lax.rem(row // 2, NY)
    z = row // (2 * NY)

    def rid(zz, yy, cc):
        return (lax.rem(zz, NZ) * NY + lax.rem(yy, NY)) * 2 + cc

    sib = rid(z, y, 1 - core)
    peers = {
        ("y", 1): rid(z, y + 1, core),
        ("y", -1): rid(z, y + NY - 1, core),
        ("z", 1): rid(z + 1, y, core),
        ("z", -1): rid(z + NZ - 1, y, core),
    }
    own_d = pltpu.make_async_copy(dens, dg.at[row], dens_sem.at[0])
    own_e = pltpu.make_async_copy(extra, eg.at[row], dens_sem.at[1])
    own_d.start()
    own_e.start()

    def chip_of(t):
        dy, dz = pick(t, [o[0] for o in ORDER]), pick(t, [o[1] for o in ORDER])
        return lax.rem(z + dz, NZ) * NY + lax.rem(y + dy, NY), dy, dz

    def vir_copy(t):
        q, _, _ = chip_of(t)
        return pltpu.make_async_copy(
            vir.at[:, pl.ds(pl.multiple_of(q * 1024, 1024), 1024)], cbuf.at[q], vir_sem.at[t])

    def start_vir(t, _):
        vir_copy(t).start()
        return 0

    barrier = pltpu.get_barrier_semaphore()
    targets = [(p, ax) for p in peers.values()] + [(sib, ax)]
    targets += [(row, lax.rem(ax + k, NX)) for k in range(1, NX)]
    for target in targets:
        pl.semaphore_signal(barrier, inc=1, device_id=target, device_id_type=pl.DeviceIdType.MESH)
    pl.semaphore_wait(barrier, len(targets))
    own_d.wait()
    own_e.wait()

    def gather(units, recv, compute, before):
        def send(k, r, target):
            ref_of, sem, _, _ = units[k]
            pltpu.make_async_remote_copy(
                ref_of(r), ref_of(r), sem, recv.at[k, r],
                device_id=(target, ax), device_id_type=pl.DeviceIdType.MESH).start()

        def wait(k, r):
            ref_of, sem, _, _ = units[k]
            pltpu.make_async_remote_copy(
                ref_of(r), ref_of(r), sem, recv.at[k, r],
                device_id=(sib, ax), device_id_type=pl.DeviceIdType.MESH).wait_recv()

        other = {"y": "z", "z": "y"}
        n = len(units)
        for phase in range(2):
            for k in range(n):
                axis = units[k][2] if phase == 0 else other[units[k][2]]
                send(k, row, peers[(axis, 1)])
                send(k, row, peers[(axis, -1)])
        for k in range(n):
            send(k, row, sib)
        before()

        def step(t, _):
            @pl.when(t < NCHIP)
            def _():
                q, dy, dz = chip_of(t)
                r = q * 2 + core
                for k in range(n):
                    _, _, axis, sgn = units[k]
                    du, dv = (dy, dz) if axis == "y" else (dz, dy)
                    back = NY - 1 if sgn == 1 else 1
                    wait(k, r)

                    @pl.when((du == back) & (dv == 0))
                    def _():
                        send(k, r, peers[(axis, sgn)])

                    @pl.when(dv == 0)
                    def _():
                        send(k, r, peers[(other[axis], 1)])
                        send(k, r, peers[(other[axis], -1)])

                    @pl.when(dv == back)
                    def _():
                        send(k, r, peers[(other[axis], sgn)])

                for k in range(n):
                    send(k, r, sib)

            q, _, _ = chip_of(t - 1)
            for k in range(n):
                wait(k, q * 2 + 1 - core)
            compute(t - 1, q)
            return 0

        lax.fori_loop(1, NCHIP + 1, step, 0)

    def rows_of(buf, k):
        return lambda r: buf.at[r, pl.ds(64 * k, 64)]

    shape_of = [("y", 1), ("z", 1), ("y", -1), ("z", -1)]
    d_units = [(rows_of(dg, k), d_send.at[k]) + shape_of[k] for k in range(UNITS)]
    d_units.append((lambda r: eg.at[r], e_send.at[0], "y", 1))
    h_units = [(rows_of(hg, k), h_send.at[k]) + shape_of[k] for k in range(UNITS)]

    def before_d():
        lax.fori_loop(0, NCHIP, start_vir, 0)
        acc[...] = jnp.zeros_like(acc)
        spread[...] = (iota((128, 256), 0) == iota((128, 256), 1) // PAD).astype(F32).astype(BF16)

    def compute_d(t, q):
        vir_copy(t).wait()
        part = dot_nt(dg[2 * q], cbuf[q, :, 0:512]) + dot_nt(dg[2 * q + 1], cbuf[q, :, 512:1024])
        for b in range(4):
            acc[b] += part[:, 128 * b:128 * b + 128]

    gather(d_units, d_recv, compute_d, before_d)

    for i in range(OCC):
        for b in range(4):
            hg[row, 32 * i:32 * i + 32, 128 * b:128 * b + 128] = acc[b, pl.ds(i, 32, stride=OCC), :].astype(BF16)

    def before_h():
        lens = slen[...]
        lens_f = lens.astype(F32)
        lower = (iota((64, 64), 0) < iota((64, 64), 1)).astype(F32).astype(BF16)
        starts = dot(lens_f.astype(BF16), lower)
        vtab[0, :, 0:64] = (starts * 32.0 + lens_f).astype(I32)
        meta = eg[:, 8:10, :].astype(F32)
        own = meta[:, 0, 0:256]
        nu = meta[:, 0, 256:512]
        code = meta[:, 1, 0:256] * 4096.0 + meta[:, 1, 256:512] * 64.0 + nu + 131072.0
        match = own == row.astype(F32)
        match_f = match.astype(F32)
        upper = (iota((256, 256), 0) < iota((256, 256), 1)).astype(F32).astype(BF16)
        rank = dot(match_f.astype(BF16), upper)
        lane = iota((NROW, 128), 1)
        table = jnp.zeros((NROW, 128), F32)
        for r in range(CAP):
            val = jnp.sum(jnp.where(match & (rank == float(r)), code, 0.0), axis=1, keepdims=True)
            table = jnp.where(lane == r, val, table)
        vtab[1] = table.astype(I32)
        c0 = pltpu.make_async_copy(vtab.at[0], stab, t_sem.at[0])
        c1 = pltpu.make_async_copy(vtab.at[1], ptab, t_sem.at[1])
        c0.start()
        c1.start()
        for r in range(NROW):
            piece = eg[r, 0:8, :].astype(F32)
            for b in range(4):
                occf[4 * r + b] = piece[:, 128 * b:128 * b + 128]
        c0.wait()
        c1.wait()

    lane8 = iota((8, 128), 1)
    lane256 = iota((1, 256), 1)

    def blocks(j):
        target = jnp.full((1, 256), -1, I32)
        for r in range(CAP):
            v = ptab[j, r]
            live = (v >> 17) & 1
            nu_w = stab[j, v & 63]
            rho = (v >> 12) & 31
            mu_w = stab[rho, (v >> 6) & 63]
            q0 = (mu_w >> 5) & 511
            mu_len = (mu_w & 31) * live
            n0 = (nu_w >> 5) & 511
            nu_len = (nu_w & 31) * live
            b = q0 >> 7
            off = q0 & 127
            left = occf[rho * 4 + b]
            right = occf[rho * 4 + jnp.minimum(b + 1, 3)]
            shift = (128 - off) & 127
            tile = jnp.where(lane8 < 128 - off, pltpu.roll(left, shift, 1), pltpu.roll(right, shift, 1))
            rolled[8 * r:8 * r + 8, :] = jnp.where(lane8 < mu_len, tile, 0.0)
            inner = lane256 - r * PAD
            target = jnp.where((inner >= 0) & (inner < nu_len), inner + n0, target)
        cexp[...] = dot(rolled[...].astype(BF16), spread[...])
        select = (iota((512, 256), 0) == target).astype(F32).astype(BF16)
        tiles = dot(hg[j], select)
        lane = iota((32, 128), 1)
        mask_n = (iota((PAD, 256), 0) == iota((PAD, 256), 1) % PAD).astype(F32)
        for g in range(2):
            xs = [tiles[32 * i:32 * i + 32, 128 * g:128 * g + 128] for i in range(OCC)]
            for bit in (1, 2, 4):
                low = (lane // (PAD * bit)) % 2 == 0
                ys = list(xs)
                for i in range(OCC):
                    if i & bit:
                        continue
                    a, c = xs[i], xs[i | bit]
                    ys[i] = jnp.where(low, a, pltpu.roll(c, PAD * bit, 1))
                    ys[i | bit] = jnp.where(low, pltpu.roll(a, 128 - PAD * bit, 1), c)
                xs = ys
            for s in range(8):
                slot = 8 * g + s
                coeff = jnp.concatenate(
                    [(cexp[8 * slot + i:8 * slot + i + 1, :] * mask_n).astype(BF16) for i in range(OCC)], axis=0)
                block = dot(xs[s].astype(BF16), coeff).astype(BF16)
                out[j * CAP + slot] = block
                wide = block.astype(F32)
                sq = wide * wide
                sq = sq[:, 0:128] + sq[:, 128:256]
                squares[j, slot:slot + 1, :] = jnp.sum(sq, axis=0, keepdims=True)

    def compute_h(t, q):
        def one(c, _):
            blocks(2 * q + c)
            return 0

        lax.fori_loop(0, 2, one, 0)

    gather(h_units, h_recv, compute_h, before_h)

    diag = iota((128, 128), 0) == iota((128, 128), 1)
    for b in range(4):
        part = squares[8 * b:8 * b + 8].reshape(128, 128)
        lanes = jnp.sum(part, axis=1, keepdims=True)
        sumout[b:b + 1, :] = jnp.sum(jnp.where(diag, lanes, 0.0), axis=0, keepdims=True)
    sumout[4:8, :] = jnp.zeros((4, 128), F32)
    sumbuf[ax] = sumout[...]
    copies = []
    for k in range(1, NX):
        peer = lax.rem(ax + k, NX)
        copy = pltpu.make_async_remote_copy(
            sumout, sumbuf.at[ax], x_send.at[k], x_recv.at[k],
            device_id=(row, peer), device_id_type=pl.DeviceIdType.MESH)
        copy.start()
        copies.append(copy)
    for copy in copies:
        copy.wait_recv()
    total_out[...] = (sumbuf[0] + sumbuf[1]) + (sumbuf[2] + sumbuf[3])
    for copy in copies:
        copy.wait_send()
    for k in range(UNITS):
        for buf, sem in ((dg, d_send), (hg, h_send)):
            ref = buf.at[pl.ds(0, 31), pl.ds(64 * k, 64)]
            pltpu.make_async_copy(ref, ref, sem.at[k]).wait()
    ref = eg.at[pl.ds(0, 31)]
    pltpu.make_async_copy(ref, ref, e_send.at[0]).wait()


def per_device(density, vir_coeffs, occ_coeffs, shell_len, mu_shell, nu_shell, owner):
    dens = density.reshape(256, 512)
    meta = jnp.concatenate([owner[:, 0], nu_shell, mu_shell // 64, mu_shell % 64]).reshape(2, 512).astype(BF16)
    extra = jnp.concatenate([occ_coeffs, meta, jnp.zeros((6, 512), BF16)], axis=0)
    vmem = pl.BlockSpec(memory_space=pltpu.VMEM)
    hbm = pl.BlockSpec(memory_space=pl.ANY)
    blocks, total = pl.pallas_call(
        kernel,
        out_shape=(pltpu.VMEM((512, 32, 256), BF16), jax.ShapeDtypeStruct((8, 128), F32)),
        in_specs=[hbm, hbm, hbm, vmem],
        out_specs=(pl.BlockSpec(memory_space=pltpu.VMEM), vmem),
        scratch_shapes=[
            pltpu.VMEM((NROW, 256, 512), BF16),
            pltpu.VMEM((NROW, 256, 512), BF16),
            pltpu.VMEM((NCHIP, 512, 1024), BF16),
            pltpu.VMEM((NROW, 16, 512), BF16),
            pltpu.VMEM((4, 256, 128), F32),
            pltpu.VMEM((4 * NROW, 8, 128), F32),
            pltpu.VMEM((128, 256), BF16),
            pltpu.VMEM((128, 128), F32),
            pltpu.VMEM((128, 256), F32),
            pltpu.VMEM((NROW, CAP, 128), F32),
            pltpu.VMEM((NX, 8, 128), F32),
            pltpu.VMEM((8, 128), F32),
            pltpu.VMEM((2, NROW, 128), I32),
            pltpu.SMEM((NROW, 128), I32),
            pltpu.SMEM((NROW, 128), I32),
            pltpu.SemaphoreType.DMA((2,)),
            pltpu.SemaphoreType.DMA((NCHIP,)),
            pltpu.SemaphoreType.DMA((UNITS + 1, NROW)),
            pltpu.SemaphoreType.DMA((UNITS, NROW)),
            pltpu.SemaphoreType.DMA((UNITS,)),
            pltpu.SemaphoreType.DMA((UNITS,)),
            pltpu.SemaphoreType.DMA((1,)),
            pltpu.SemaphoreType.DMA((NX,)),
            pltpu.SemaphoreType.DMA((NX,)),
            pltpu.SemaphoreType.DMA((2,)),
        ],
        compiler_params=pltpu.CompilerParams(
            collective_id=0, has_side_effects=True, vmem_limit_bytes=48 * 1024 * 1024),
    )(dens, vir_coeffs, extra, shell_len)
    pair_scale = jnp.sqrt(total[0:4].reshape(512) / (128 * PAD * PAD) + 1e-06)
    return blocks, pair_scale


def solution(mesh):
    return jax.shard_map(
        per_device,
        mesh=mesh,
        in_specs=(
            P("aux", None, "rows"),
            P("rows", None),
            P(None, "rows"),
            P(),
            P("rows"),
            P("rows"),
            P("rows", None),
        ),
        out_specs=(P("rows", "aux", None), P("rows")),
        check_vma=False,
    )
```

time: 330 us -> 104 us (0.32); the launches traced: 326 us -> 103 us
  blocking collectives: 139 us -> 0 us
  local copies, waits for them, and re-layouts: 124 us -> 3.5 us
  Pallas kernels: 0 us -> 94.8 us
  matrix products: 37.4 us -> 0 us
  between operations: 14.2 us -> 0.65 us
  other arithmetic: 10.5 us -> 4.05 us
    all_to_all x1 -> x0, blocking collectives: 98.1 us -> none  [per_device(): lax.all_to_all(outgoing, 'rows', split_axis=0, concat_axis=0, tiled=True)]
    pallas_call x0 -> x1, Pallas kernels: none -> 94.8 us  [per_device(): pl.pallas_call(kernel, out_shape=(pltpu.VMEM((512, 32, 256), BF16), jax.S...]
    convert_element_type x1, local copies, waits for them, and re-layouts: 48.5 us -> 0.01 us  [per_device(): jnp.concatenate([owner[:, 0], nu_shell, mu_shell // 64, mu_shell % 64])]
    dot_general x3 -> x0, matrix products: 37.4 us -> none  [the longest x1 19.8 us: per_device(): jnp.einsum('ism,pisn->spmn', coeff_slots.reshape(occupied, slot_total, PA...]
    reshape x2 -> x0, local copies, waits for them, and re-layouts: 32.3 us -> none  [the longest x1 17.7 us: per_device(): half_slots.reshape(local_aux, occupied, slot_total, PAD)]
    all_gather x1 -> x0, blocking collectives: 30.7 us -> none  [per_device(): occ_full = lax.all_gather(occ_coeffs, 'rows', axis=1, tiled=True)]
    gather x2 -> x0, local copies, waits for them, and re-layouts: 25.6 us -> none  [per_device(): jnp.take(occ_pad, mu_column, axis=1)]
    psum x1 -> x0, blocking collectives: 10.5 us -> none  [per_device(): total = lax.psum(partial_squares, 'aux')]
  transfers between devices with their start and end apart: 1 -> 0, of which waited for: 0 -> 0; matrix products, arithmetic and copies ran while one was open for 12% -> 0% of each run, Pallas kernels for 0% -> 0%
where the time goes in v1:
time: 104 us; the launch traced here: 103 us
  Pallas kernels  94.8 us (91%)
  other arithmetic  4.05 us (4%)
  local copies, waits for them, and re-layouts  3.5 us (3%)
    pallas_call x1, Pallas kernels, per_device(): pl.pallas_call(kernel, out_shape=(pltpu.VMEM((512, 32, 256), BF16), jax.S...  94.8 us
    unnamed x3, local copies, waits for them, and re-layouts  3.4 us

profile of v1, /device:TPU:24, one launch (start us, length us, event | category | flops | bytes accessed | tf_op | source)
XLA Modules:
  0.0 103.0 jit_solution(15709905478762252036)
XLA Ops:
  0.6 0.7 convert.14
  1.3 0.7 convert_reduce_fusion
  2.0 0.1 pad.2.clone
  2.1 0.7 fusion.1
  2.8 1.4 %maximum_maximum_fusion.extra = bf16[16,512]{1,0:T(8,128)(2,1)} fusion(bf16[2,512]{1,0:T(2,128)(2,1)S(1)} %convert_element_type.4, bf16[8,512]{1,0:T(8,128)(2,1)} %param.9, bf16[16]{0:T(256)(128)(2,1)S(1)} %pad.2.clone), kind=kLoop, calls=%fused_computation | loop fusion | flops 49152 | bytes 26656 | tf_op jit(solution)/shard_map/concatenate | solution.py:297
  4.2 94.8 %shard_map.86 = (bf16[512,32,256]{2,1,0:T(8,128)(2,1)S(1)}, f32[8,128]{1,0:T(8,128)}) custom-call(bf16[256,512]{1,0:T(8,128)(2,1)} %bitcast.3, bf16[512,16384]{1,0:T(8,128)(2,1)} %vir.1, bf16[16,512]{1,0:T(8,128)(2,1)} %maximum_maximum_fusion.extra, s32[32,64]{1,0:T(8,128)} %slen.1), custom_call_target="tpu_custom_call" | custom-call | tf_op jit(solution)/shard_map/pallas_call | solution.py:300
  99.0 0.0 copy-start
  99.0 3.4 %copy.10 = bf16[512,32,256]{2,1,0:T(8,128)(2,1)} copy(bf16[512,32,256]{2,1,0:T(8,128)(2,1)S(1)} %get-tuple-element.8) | data formatting | bytes 16777216
  102.4 0.0 copy-done
  102.4 0.6 sqrt_bitcast_fusion
  (3 shorter events, 0.0 us)
Async XLA Ops:
  99.0 3.4 %copy-start = (f32[8,128]{1,0:T(8,128)S(1)}, f32[8,128]{1,0:T(8,128)}, u32[]{:S(2)}) copy-start(f32[8,128]{1,0:T(8,128)} %get-tuple-element.5) | copy-start | bytes 12292

commit v2 on v1

v2 whole, which is shorter than its diff:
```python
import jax
import jax.numpy as jnp
from jax import lax
from jax.experimental import pallas as pl
from jax.experimental.pallas import tpu as pltpu
from jax.sharding import PartitionSpec as P

NY = 4
NZ = 4
NCHIP = NY * NZ
NROW = 2 * NCHIP
NX = 4
UNITS = 4
OCC = 8
PAD = 16
CAP = 16
F32 = jnp.float32
BF16 = jnp.bfloat16
I32 = jnp.int32
ROUNDS = [(3, 0), (1, 0), (0, 3), (0, 1), (2, 0), (3, 3), (3, 1), (1, 3), (1, 1), (0, 2), (2, 3), (2, 1), (3, 2), (1, 2), (2, 2)]
COMPUTE = [(0, 0), (1, 0), (3, 0), (0, 1), (0, 3), (3, 3), (1, 1), (3, 1), (1, 3), (2, 0), (0, 2), (3, 2), (2, 3), (1, 2), (2, 1), (2, 2)]
COUNTS = [1, 0, 0, 2, 1, 1, 1, 0, 1, 1, 1, 2, 2, 2, 1]


def iota(shape, dim):
    return lax.broadcasted_iota(I32, shape, dim)


def dot(a, b):
    return lax.dot_general(a, b, (((1,), (0,)), ((), ())), preferred_element_type=F32)


def dot_nt(a, b):
    return lax.dot_general(a, b, (((1,), (1,)), ((), ())), preferred_element_type=F32)


def packed(values, bits=2):
    word = 0
    for k, v in enumerate(values):
        word |= (v % (1 << bits)) << (bits * k)
    return jnp.int32(word - (1 << 32) if word >= 1 << 31 else word)


def entry(word, t, bits=2):
    return lax.shift_right_logical(word, bits * t) & ((1 << bits) - 1)


def kernel(dens, vir, occ, slen_h, mu_h, nu_h, own_h, out, total_out,
           dg, hg, cbuf, eo, em, slen, acc, occf, spread, repeat, rolled, cexp, targets, squares, sumbuf, sumout, vtab, wtab,
           stab, ptab,
           in_sem, vir_sem, d_recv, h_recv, o_recv, m_recv, d_send, h_send, o_send, m_send, x_recv, x_send, t_sem):
    row = lax.axis_index("rows")
    ax = lax.axis_index("aux")
    core = lax.rem(row, 2)
    y = lax.rem(row // 2, NY)
    z = row // (2 * NY)

    def rid(zz, yy, cc):
        return (lax.rem(zz, NZ) * NY + lax.rem(yy, NY)) * 2 + cc

    sib = rid(z, y, 1 - core)
    peers = {
        ("y", 1): rid(z, y + 1, core),
        ("y", -1): rid(z, y + NY - 1, core),
        ("z", 1): rid(z + 1, y, core),
        ("z", -1): rid(z + NZ - 1, y, core),
    }
    fills = [(dens, dg.at[row]), (occ, eo.at[row]), (own_h, em.at[row, pl.ds(0, 2)]),
             (mu_h, em.at[row, pl.ds(2, 2)]), (nu_h, em.at[row, pl.ds(4, 2)]), (slen_h, slen)]
    fills = [pltpu.make_async_copy(src, dst, in_sem.at[k]) for k, (src, dst) in enumerate(fills)]
    for fill in fills:
        fill.start()

    comp_y, comp_z = packed([o[0] for o in COMPUTE]), packed([o[1] for o in COMPUTE])
    round_a, round_b = packed([o[0] for o in ROUNDS]), packed([o[1] for o in ROUNDS])
    counts = packed(COUNTS)

    def chip_of(t):
        return lax.rem(z + entry(comp_z, t), NZ) * NY + lax.rem(y + entry(comp_y, t), NY)

    def vir_copy(t):
        q = chip_of(t)
        return pltpu.make_async_copy(
            vir.at[:, pl.ds(pl.multiple_of(q * 1024, 1024), 1024)], cbuf.at[q], vir_sem.at[t])

    def start_vir(t, _):
        vir_copy(t).start()
        return 0

    barrier = pltpu.get_barrier_semaphore()
    greeted = [(p, ax) for p in peers.values()] + [(sib, ax)]
    greeted += [(row, lax.rem(ax + k, NX)) for k in range(1, NX)]
    for target in greeted:
        pl.semaphore_signal(barrier, inc=1, device_id=target, device_id_type=pl.DeviceIdType.MESH)
    acc[...] = jnp.zeros_like(acc)
    spread[...] = (iota((128, 256), 0) == iota((128, 256), 1) // PAD).astype(F32).astype(BF16)
    occf[4 * NROW] = jnp.zeros((8, 128), F32)
    for k in range(4):
        col = iota((128, 256), 1)
        repeat[k] = (iota((128, 256), 0) == (2 * k + col // 128) * PAD + col % PAD).astype(F32).astype(BF16)
    for fill in fills:
        fill.wait()
    pl.semaphore_wait(barrier, len(greeted))

    def gather(units, compute, before):
        def send(k, r, target):
            ref_of, sem, recv, _, _ = units[k]
            pltpu.make_async_remote_copy(
                ref_of(r), ref_of(r), sem, recv.at[r],
                device_id=(target, ax), device_id_type=pl.DeviceIdType.MESH).start()

        def wait(k, r):
            ref_of, sem, recv, _, _ = units[k]
            pltpu.make_async_remote_copy(
                ref_of(r), ref_of(r), sem, recv.at[r],
                device_id=(sib, ax), device_id_type=pl.DeviceIdType.MESH).wait_recv()

        other = {"y": "z", "z": "y"}
        n = len(units)
        for phase in range(2):
            for k in range(n):
                axis = units[k][3] if phase == 0 else other[units[k][3]]
                send(k, row, peers[(axis, 1)])
                send(k, row, peers[(axis, -1)])
        for k in range(n):
            send(k, row, sib)
        before()

        def step(t, done):
            a, b = entry(round_a, t), entry(round_b, t)
            for k in range(n):
                axis, sgn = units[k][3], units[k][4]
                if sgn == 1:
                    du, dv = a, b
                else:
                    du, dv = jnp.where(b == 0, lax.rem(4 - a, 4), a), lax.rem(4 - b, 4)
                dy, dz = (du, dv) if axis == "y" else (dv, du)
                r = rid(z + dz, y + dy, core)
                wait(k, r)

                @pl.when((a == 3) & (b == 0))
                def _():
                    send(k, r, peers[(axis, sgn)])

                @pl.when(b == 0)
                def _():
                    send(k, r, peers[(other[axis], 1)])
                    send(k, r, peers[(other[axis], -1)])

                @pl.when(b == 3)
                def _():
                    send(k, r, peers[(other[axis], sgn)])

                send(k, r, sib)

            def one(c, _):
                q = chip_of(c)
                for k in range(n):
                    wait(k, q * 2 + 1 - core)
                compute(c, q)
                return 0

            last = done + entry(counts, t)
            lax.fori_loop(done, last, one, 0)
            return last

        lax.fori_loop(0, NCHIP - 1, step, jnp.int32(0))

    def rows_of(buf, k):
        return lambda r: buf.at[r, pl.ds(64 * k, 64)]

    shape_of = [("y", 1), ("z", 1), ("y", -1), ("z", -1)]
    d_units = [(rows_of(dg, k), d_send.at[k], d_recv.at[k]) + shape_of[k] for k in range(UNITS)]
    d_units.append((lambda r: eo.at[r], o_send.at[0], o_recv, "y", 1))
    d_units.append((lambda r: em.at[r], m_send.at[0], m_recv, "z", 1))
    h_units = [(rows_of(hg, k), h_send.at[k], h_recv.at[k]) + shape_of[k] for k in range(UNITS)]

    def before_d():
        lax.fori_loop(0, NCHIP, start_vir, 0)

    def compute_d(t, q):
        vir_copy(t).wait()
        part = dot_nt(dg[2 * q], cbuf[q, :, 0:512]) + dot_nt(dg[2 * q + 1], cbuf[q, :, 512:1024])
        for b in range(4):
            acc[b] += part[:, 128 * b:128 * b + 128]

    gather(d_units, compute_d, before_d)

    for i in range(OCC):
        for b in range(4):
            hg[row, 32 * i:32 * i + 32, 128 * b:128 * b + 128] = acc[b, pl.ds(i, 32, stride=OCC), :].astype(BF16)

    def before_h():
        lens = slen[...]
        lens_f = lens.astype(F32)
        lower = (iota((64, 64), 0) < iota((64, 64), 1)).astype(F32).astype(BF16)
        starts = dot(lens_f.astype(BF16), lower)
        starts_i = starts.astype(I32)
        tile = iota((NROW, 64), 0) * 4 + (starts_i >> 7)
        vtab[0:NROW, 0:64] = tile | ((starts_i & 127) << 7) | (lens << 14)
        vtab[NROW:NROW + 8, :] = jnp.zeros((8, 128), I32)
        meta = em[...]
        own = jnp.concatenate([meta[:, 0, :], meta[:, 1, :]], axis=1)
        mu = jnp.concatenate([meta[:, 2, :], meta[:, 3, :]], axis=1)
        nu = jnp.concatenate([meta[:, 4, :], meta[:, 5, :]], axis=1)
        match = own == row
        upper = (iota((256, 256), 0) < iota((256, 256), 1)).astype(F32).astype(BF16)
        rank = dot(match.astype(F32).astype(BF16), upper)
        code = ((mu - 64 * NROW) * 64 + nu).astype(F32)
        lane = iota((NROW, 128), 1)
        table = jnp.zeros((NROW, 128), F32)
        for r in range(CAP):
            val = jnp.sum(jnp.where(match & (rank == float(r)), code, 0.0), axis=1, keepdims=True)
            table = jnp.where(lane == r, val, table)
        table = table.astype(I32) + 64 * 64 * NROW
        wtab[...] = table >> 6
        c0 = pltpu.make_async_copy(vtab, stab, t_sem.at[0])
        c1 = pltpu.make_async_copy(wtab, ptab, t_sem.at[1])
        c0.start()
        c1.start()
        live = table < 64 * 64 * NROW
        nus = table & 63
        words = jnp.concatenate([starts_i * 32 + lens, jnp.zeros((NROW, 64), I32)], axis=1)
        word = jnp.where(live, jnp.take_along_axis(words, nus, axis=1), 0)
        n0i = word >> 5
        nl = word & 31
        parts = [n0i >> 6, n0i & 63, nl]
        hi, lo, ln = [dot(p.astype(F32).astype(BF16), spread[...]) for p in parts]
        inner = (iota((NROW, 256), 1) & (PAD - 1)).astype(F32)
        targets[...] = jnp.where(inner < ln, hi * 64.0 + lo + inner, -1.0)
        for r in range(NROW):
            piece = eo[r].astype(F32)
            for b in range(4):
                occf[4 * r + b] = piece[:, 128 * b:128 * b + 128]
        c0.wait()
        c1.wait()
        lane8 = iota((8, 128), 1)

        def coeffs(j, _):
            for r in range(CAP):
                g = ptab[j, r]
                w = stab[jnp.minimum((g >> 6) & 63, NROW), g & 63]
                tile = w & 127
                off = (w >> 7) & 127
                shift = (128 - off) & 127
                left = pltpu.roll(occf[tile], shift, 1)
                right = pltpu.roll(occf[tile + 1], shift, 1)
                both = jnp.where(lane8 < 128 - off, left, right)
                rolled[8 * r:8 * r + 8, :] = jnp.where(lane8 < (w >> 14), both, 0.0)
            cexp[j] = dot(rolled[...].astype(BF16), spread[...])
            return 0

        lax.fori_loop(0, NROW, coeffs, 0)

    def blocks(j):
        select = (iota((512, 256), 0).astype(F32) == targets[pl.ds(j, 1), :]).astype(F32).astype(BF16)
        tiles = dot(hg[j], select)
        tiles = tiles.astype(BF16)
        for pair in range(CAP // 2):
            g = pair // 4
            wide_tile = dot(tiles[:, 128 * g:128 * g + 128], repeat[pair % 4])
            for s in range(2):
                slot = 2 * pair + s
                acc0 = acc1 = None
                for i in range(OCC):
                    tile = wide_tile[32 * i:32 * i + 32, 128 * s:128 * s + 128]
                    row_c = cexp[j, OCC * slot + i:OCC * slot + i + 1, :]
                    t0, t1 = tile * row_c[:, 0:128], tile * row_c[:, 128:256]
                    acc0 = t0 if i == 0 else acc0 + t0
                    acc1 = t1 if i == 0 else acc1 + t1
                sq = None
                for h, part in enumerate((acc0, acc1)):
                    block = part.astype(BF16)
                    out[j * CAP + slot, :, 128 * h:128 * h + 128] = block
                    wide = block.astype(F32)
                    sq = wide * wide if h == 0 else sq + wide * wide
                squares[j, slot:slot + 1, :] = jnp.sum(sq, axis=0, keepdims=True)

    def compute_h(t, q):
        for c in range(2):
            blocks(2 * q + c)

    gather(h_units, compute_h, before_h)

    diag = iota((128, 128), 0) == iota((128, 128), 1)
    for b in range(4):
        part = squares[8 * b:8 * b + 8].reshape(128, 128)
        lanes = jnp.sum(part, axis=1, keepdims=True)
        sumout[b:b + 1, :] = jnp.sum(jnp.where(diag, lanes, 0.0), axis=0, keepdims=True)
    sumout[4:8, :] = jnp.zeros((4, 128), F32)
    sumbuf[ax] = sumout[...]
    copies = []
    for k in range(1, NX):
        peer = lax.rem(ax + k, NX)
        copy = pltpu.make_async_remote_copy(
            sumout, sumbuf.at[ax], x_send.at[k], x_recv.at[k],
            device_id=(row, peer), device_id_type=pl.DeviceIdType.MESH)
        copy.start()
        copies.append(copy)
    for k in range(UNITS):
        for buf, sem in ((dg, d_send), (hg, h_send)):
            ref = buf.at[pl.ds(0, 31), pl.ds(64 * k, 64)]
            pltpu.make_async_copy(ref, ref, sem.at[k]).wait()
    for buf, sem in ((eo, o_send), (em, m_send)):
        ref = buf.at[pl.ds(0, 31)]
        pltpu.make_async_copy(ref, ref, sem.at[0]).wait()
    for copy in copies:
        copy.wait_recv()
    total_out[...] = (sumbuf[0] + sumbuf[1]) + (sumbuf[2] + sumbuf[3])
    for copy in copies:
        copy.wait_send()


def per_device(density, vir_coeffs, occ_coeffs, shell_len, mu_shell, nu_shell, owner):
    hbm = pl.BlockSpec(memory_space=pl.ANY)
    vmem = pl.BlockSpec(memory_space=pltpu.VMEM)
    dma = pltpu.SemaphoreType.DMA
    blocks, total = pl.pallas_call(
        kernel,
        out_shape=(pltpu.VMEM((512, 32, 256), BF16), pltpu.VMEM((8, 128), F32)),
        in_specs=[hbm] * 7,
        out_specs=(vmem, vmem),
        scratch_shapes=[
            pltpu.VMEM((NROW, 256, 512), BF16),
            pltpu.VMEM((NROW, 256, 512), BF16),
            pltpu.VMEM((NCHIP, 512, 1024), BF16),
            pltpu.VMEM((NROW, 8, 512), BF16),
            pltpu.VMEM((NROW, 8, 128), I32),
            pltpu.VMEM((NROW, 64), I32),
            pltpu.VMEM((4, 256, 128), F32),
            pltpu.VMEM((4 * NROW + 1, 8, 128), F32),
            pltpu.VMEM((128, 256), BF16),
            pltpu.VMEM((4, 128, 256), BF16),
            pltpu.VMEM((128, 128), F32),
            pltpu.VMEM((NROW, 128, 256), F32),
            pltpu.VMEM((NROW, 256), F32),
            pltpu.VMEM((NROW, CAP, 128), F32),
            pltpu.VMEM((NX, 8, 128), F32),
            pltpu.VMEM((8, 128), F32),
            pltpu.VMEM((NROW + 8, 128), I32),
            pltpu.VMEM((NROW, 128), I32),
            pltpu.SMEM((NROW + 8, 128), I32),
            pltpu.SMEM((NROW, 128), I32),
            dma((6,)), dma((NCHIP,)), dma((UNITS, NROW)), dma((UNITS, NROW)), dma((NROW,)), dma((NROW,)),
            dma((UNITS,)), dma((UNITS,)), dma((1,)), dma((1,)), dma((NX,)), dma((NX,)), dma((2,)),
        ],
        compiler_params=pltpu.CompilerParams(
            collective_id=0, has_side_effects=True, vmem_limit_bytes=48 * 1024 * 1024),
    )(density.reshape(256, 512), vir_coeffs, occ_coeffs, shell_len,
      mu_shell.reshape(2, 128), nu_shell.reshape(2, 128), owner.reshape(2, 128))
    pair_scale = jnp.sqrt(total[0:4].reshape(512) / (128 * PAD * PAD) + 1e-06)
    return blocks, pair_scale


def solution(mesh):
    return jax.shard_map(
        per_device,
        mesh=mesh,
        in_specs=(
            P("aux", None, "rows"),
            P("rows", None),
            P(None, "rows"),
            P(),
            P("rows"),
            P("rows"),
            P("rows", None),
        ),
        out_specs=(P("rows", "aux", None), P("rows")),
        check_vma=False,
    )
```

time: 104 us -> 91.3 us (0.88)
  Pallas kernels: 94.8 us -> 85.4 us
  other arithmetic: 4.05 us -> 0.59 us
    pallas_call x1, Pallas kernels: 94.8 us -> 85.4 us  [per_device(): pl.pallas_call(kernel, out_shape=(pltpu.VMEM((512, 32, 256), BF16), pltpu...]
    another operation x3 -> x0, other arithmetic: 2.07 us -> none
    concatenate x2 -> x0, other arithmetic: 1.39 us -> none  [the longest x1 1.38 us: per_device(): jnp.concatenate([occ_coeffs, meta, jnp.zeros((6, 512), BF16)], axis=0)]
    unnamed x3 -> x1, local copies, waits for them, and re-layouts: 3.4 us -> 3.4 us
where the time goes in v2:
time: 91.3 us; the launch traced here: 90.1 us
  Pallas kernels  85.4 us (94%)
  local copies, waits for them, and re-layouts  3.4 us (4%)
    pallas_call x1, Pallas kernels, per_device(): pl.pallas_call(kernel, out_shape=(pltpu.VMEM((512, 32, 256), BF16), pltpu...  85.4 us
    unnamed x1, local copies, waits for them, and re-layouts  3.4 us

profile of v2, /device:TPU:24, one launch (start us, length us, event | category | flops | bytes accessed | tf_op | source)
XLA Modules:
  0.0 90.1 jit_solution(13396188782213612173)
XLA Ops:
  0.6 85.4 %shard_map.86 = (bf16[512,32,256]{2,1,0:T(8,128)(2,1)S(1)}, f32[8,128]{1,0:T(8,128)S(1)}) custom-call(bf16[256,512]{1,0:T(8,128)(2,1)} %bitcast.6, bf16[512,16384]{1,0:T(8,128)(2,1)} %vir.1, bf16[8,512]{1,0:T(8,128)(2,1)} %occ.1, s32[32,64]{1,0:T(8,128)} %slen_h.1, s32[2,128]{1,0:T(2,128)} %bitcast.7, s32[2,128]{1,0:T(2,128)} %bitcast.8, s32[2,128]{1,0:T(2,128)} %bitcast.9), custom_call_target="tpu_custom_call" | custom-call | tf_op jit(solution)/shard_map/pallas_call | solution.py:318
  86.1 3.4 %copy.10 = bf16[512,32,256]{2,1,0:T(8,128)(2,1)} copy(bf16[512,32,256]{2,1,0:T(8,128)(2,1)S(1)} %get-tuple-element.6) | data formatting | bytes 16777216
  89.5 0.6 sqrt_bitcast_fusion

commit v3 on v2

v3 whole, which is shorter than its diff:
```python
import jax
import jax.numpy as jnp
from jax import lax
from jax.experimental import pallas as pl
from jax.experimental.pallas import tpu as pltpu
from jax.sharding import PartitionSpec as P

NY = 4
NZ = 4
NCHIP = NY * NZ
NROW = 2 * NCHIP
NX = 4
UNITS = 4
OCC = 8
PAD = 16
CAP = 16
F32 = jnp.float32
BF16 = jnp.bfloat16
I32 = jnp.int32
ROUNDS = [(3, 0), (1, 0), (0, 3), (0, 1), (2, 0), (3, 3), (3, 1), (1, 3), (1, 1), (0, 2), (2, 3), (2, 1), (3, 2), (1, 2), (2, 2)]
COMPUTE = [(0, 0), (1, 0), (3, 0), (0, 1), (0, 3), (3, 3), (1, 1), (3, 1), (1, 3), (2, 0), (0, 2), (3, 2), (2, 3), (1, 2), (2, 1), (2, 2)]
COUNTS_D = [1, 0, 0, 0, 0, 0, 0, 0, 0, 3, 2, 3, 2, 2, 3]
COUNTS_H = [1, 0, 0, 0, 1, 1, 1, 1, 1, 1, 1, 1, 1, 1, 5]
E_COUNT = [0, 0, 0, 0, 4, 0, 0, 0, 6, 0, 0, 0, 4, 0, 0]
E_FROM = [0, 0, 0, 0, 0, 0, 0, 0, 4, 0, 0, 0, 10, 0, 0]


def pick(t, values):
    out = jnp.int32(values[0])
    for k in range(1, len(values)):
        if values[k] != values[0]:
            out = jnp.where(t == k, jnp.int32(values[k]), out)
    return out


def iota(shape, dim):
    return lax.broadcasted_iota(I32, shape, dim)


def dot(a, b):
    return lax.dot_general(a, b, (((1,), (0,)), ((), ())), preferred_element_type=F32)


def dot_nt(a, b):
    return lax.dot_general(a, b, (((1,), (1,)), ((), ())), preferred_element_type=F32)


def packed(values, bits=2):
    word = 0
    for k, v in enumerate(values):
        word |= (v % (1 << bits)) << (bits * k)
    return jnp.int32(word - (1 << 32) if word >= 1 << 31 else word)


def entry(word, t, bits=2):
    return lax.shift_right_logical(word, bits * t) & ((1 << bits) - 1)


def kernel(dens, vir, occ, slen_h, mu_h, nu_h, own_h, out, total_out,
           dg, hg, cbuf, eo, em, slen, acc, occf, spread, lined, cexp, targets, squares, sumbuf, sumout, vtab, wtab,
           stab, ptab,
           in_sem, vir_sem, d_recv, h_recv, o_recv, m_recv, d_send, h_send, o_send, m_send, x_recv, x_send, t_sem):
    row = lax.axis_index("rows")
    ax = lax.axis_index("aux")
    core = lax.rem(row, 2)
    y = lax.rem(row // 2, NY)
    z = row // (2 * NY)

    def rid(zz, yy, cc):
        return (lax.rem(zz, NZ) * NY + lax.rem(yy, NY)) * 2 + cc

    sib = rid(z, y, 1 - core)
    peers = {
        ("y", 1): rid(z, y + 1, core),
        ("y", -1): rid(z, y + NY - 1, core),
        ("z", 1): rid(z + 1, y, core),
        ("z", -1): rid(z + NZ - 1, y, core),
    }
    fills = [(dens, dg.at[row]), (occ, eo.at[row]), (own_h, em.at[row, pl.ds(0, 2)]),
             (mu_h, em.at[row, pl.ds(2, 2)]), (nu_h, em.at[row, pl.ds(4, 2)]), (slen_h, slen)]
    fills = [pltpu.make_async_copy(src, dst, in_sem.at[k]) for k, (src, dst) in enumerate(fills)]
    for fill in fills:
        fill.start()

    comp_y, comp_z = packed([o[0] for o in COMPUTE]), packed([o[1] for o in COMPUTE])
    round_a, round_b = packed([o[0] for o in ROUNDS]), packed([o[1] for o in ROUNDS])

    def chip_of(t):
        return lax.rem(z + entry(comp_z, t), NZ) * NY + lax.rem(y + entry(comp_y, t), NY)

    def vir_copy(t):
        q = chip_of(t)
        return pltpu.make_async_copy(
            vir.at[:, pl.ds(pl.multiple_of(q * 1024, 1024), 1024)], cbuf.at[q], vir_sem.at[t])

    def start_vir(t, _):
        vir_copy(t).start()
        return 0

    barrier = pltpu.get_barrier_semaphore()
    greeted = [(p, ax) for p in peers.values()] + [(sib, ax)]
    greeted += [(row, lax.rem(ax + k, NX)) for k in range(1, NX)]
    for target in greeted:
        pl.semaphore_signal(barrier, inc=1, device_id=target, device_id_type=pl.DeviceIdType.MESH)
    acc[...] = jnp.zeros_like(acc)
    spread[...] = (iota((128, 256), 0) == iota((128, 256), 1) // PAD).astype(F32).astype(BF16)
    for fill in fills:
        fill.wait()
    pl.semaphore_wait(barrier, len(greeted))

    other = {"y": "z", "z": "y"}

    def copy_of(unit, r, target):
        ref_of, sem, recv, _, _ = unit
        return pltpu.make_async_remote_copy(
            ref_of(r), ref_of(r), sem, recv.at[r],
            device_id=(target, ax), device_id_type=pl.DeviceIdType.MESH)

    def send(unit, r, target):
        copy_of(unit, r, target).start()

    def wait(unit, r):
        copy_of(unit, r, sib).wait_recv()

    def leave(units):
        for phase in range(2):
            for unit in units:
                axis = unit[3] if phase == 0 else other[unit[3]]
                send(unit, row, peers[(axis, 1)])
                send(unit, row, peers[(axis, -1)])
        for unit in units:
            send(unit, row, sib)

    def take(unit, t):
        a, b = entry(round_a, t), entry(round_b, t)
        axis, sgn = unit[3], unit[4]
        if sgn == 1:
            du, dv = a, b
        else:
            du, dv = jnp.where(b == 0, (4 - a) & 3, a), (4 - b) & 3
        dy, dz = (du, dv) if axis == "y" else (dv, du)
        r = rid(z + dz, y + dy, core)
        wait(unit, r)

        @pl.when((a == 3) & (b == 0))
        def _():
            send(unit, r, peers[(axis, sgn)])

        @pl.when(b == 0)
        def _():
            send(unit, r, peers[(other[axis], 1)])
            send(unit, r, peers[(other[axis], -1)])

        @pl.when(b == 3)
        def _():
            send(unit, r, peers[(other[axis], sgn)])

        send(unit, r, sib)

    def gather(units, counts, compute, at_round):
        def step(t, done):
            at_round(t)
            for unit in units:
                take(unit, t)

            def one(c, _):
                q = chip_of(c)
                for unit in units:
                    wait(unit, q * 2 + 1 - core)
                compute(c, q)
                return 0

            last = done + pick(t, counts)
            lax.fori_loop(done, last, one, 0)
            return last

        lax.fori_loop(0, NCHIP - 1, step, jnp.int32(0))

    def rows_of(buf, k):
        return lambda r: buf.at[r, pl.ds(64 * k, 64)]

    shape_of = [("y", 1), ("z", 1), ("y", -1), ("z", -1)]
    d_units = [(rows_of(dg, k), d_send.at[k], d_recv.at[k]) + shape_of[k] for k in range(UNITS)]
    e_units = [(lambda r: eo.at[r], o_send.at[0], o_recv, "y", 1), (lambda r: em.at[r], m_send.at[0], m_recv, "z", -1)]
    h_units = [(rows_of(hg, k), h_send.at[k], h_recv.at[k]) + shape_of[k] for k in range(UNITS)]

    def compute_d(t, q):
        vir_copy(t).wait()
        part = dot_nt(dg[2 * q], cbuf[q, :, 0:512]) + dot_nt(dg[2 * q + 1], cbuf[q, :, 512:1024])
        for b in range(4):
            acc[b] += part[:, 128 * b:128 * b + 128]

    def tables():
        for q in range(NCHIP):
            for unit in e_units:
                wait(unit, 2 * q + 1 - core)
        lens = slen[...]
        lens_f = lens.astype(F32)
        lower = (iota((64, 64), 0) < iota((64, 64), 1)).astype(F32).astype(BF16)
        starts = dot(lens_f.astype(BF16), lower)
        starts_i = starts.astype(I32)
        tile = iota((NROW, 64), 0) * 8 + (starts_i >> 6)
        vtab[0:NROW, 0:64] = tile | (((128 - (starts_i & 63)) & 127) << 8) | (lens << 16)
        vtab[NROW:64, :] = jnp.zeros((64 - NROW, 128), I32)
        meta = em[...]
        own = jnp.concatenate([meta[:, 0, :], meta[:, 1, :]], axis=1)
        mu = jnp.concatenate([meta[:, 2, :], meta[:, 3, :]], axis=1)
        nu = jnp.concatenate([meta[:, 4, :], meta[:, 5, :]], axis=1)
        match = own == row
        upper = (iota((256, 256), 0) < iota((256, 256), 1)).astype(F32).astype(BF16)
        rank = dot(match.astype(F32).astype(BF16), upper)
        code = ((mu - 64 * NROW) * 64 + nu).astype(F32)
        lane = iota((NROW, 128), 1)
        table = jnp.zeros((NROW, 128), F32)
        for r in range(CAP):
            val = jnp.sum(jnp.where(match & (rank == float(r)), code, 0.0), axis=1, keepdims=True)
            table = jnp.where(lane == r, val, table)
        table = table.astype(I32) + 64 * 64 * NROW
        wtab[...] = ((table >> 12) << 7) | ((table >> 6) & 63)
        c0 = pltpu.make_async_copy(vtab, stab, t_sem.at[0])
        c1 = pltpu.make_async_copy(wtab, ptab, t_sem.at[1])
        c0.start()
        c1.start()
        live = table < 64 * 64 * NROW
        nus = table & 63
        words = jnp.concatenate([starts_i * 32 + lens, jnp.zeros((NROW, 64), I32)], axis=1)
        word = jnp.where(live, jnp.take_along_axis(words, nus, axis=1), 0)
        n0i = word >> 5
        nl = word & 31
        parts = [n0i >> 6, n0i & 63, nl]
        hi, lo, ln = [dot(p.astype(F32).astype(BF16), spread[...]) for p in parts]
        inner = (iota((NROW, 256), 1) & (PAD - 1)).astype(F32)
        targets[...] = jnp.where(inner < ln, hi * 64.0 + lo + inner, -1.0)
        low64 = iota((8, 128), 1) < 64
        for r in range(NROW):
            piece = eo[r].astype(F32)
            parts = [piece[:, 128 * b:128 * b + 128] for b in range(4)]
            turned = [pltpu.roll(part, 64, 1) for part in parts]
            for b in range(4):
                occf[8 * r + 2 * b] = parts[b]
                occf[8 * r + 2 * b + 1] = jnp.where(low64, turned[b], turned[b + 1] if b < 3 else 0.0)
        c0.wait()
        c1.wait()

    def coeff_rows():
        lane8 = iota((8, 128), 1)
        inner8 = lane8 & (PAD - 1)
        group8 = lane8 >> 4

        def coeffs(j, _):
            for g in range(2):
                line = jnp.zeros((8, 128), F32)
                for s in range(8):
                    pair = ptab[j, 8 * g + s]
                    w = stab[(pair >> 7) & 63, pair & 127]
                    shift = ((w >> 8) + PAD * s) & 127
                    tile = pltpu.roll(occf[w & 255], shift, 1)
                    line = jnp.where((group8 == s) & (inner8 < (w >> 16)), tile, line)
                lined[pl.ds(pl.multiple_of(8 * j, 8), 8), 128 * g:128 * g + 128] = line
            return 0

        lax.fori_loop(0, NROW, coeffs, 0)

    def expand_rows():
        lined_b = lined[...].astype(BF16)
        row256, col256 = iota((256, 256), 0), iota((256, 256), 1)
        same_slot = (row256 >> 4) == (col256 >> 4)

        def expand(n, _):
            for m in range(4):
                pick_m = (same_slot & ((row256 & (PAD - 1)) == 4 * n + m)).astype(F32).astype(BF16)
                cexp[4 * n + m] = dot(lined_b, pick_m).reshape(NROW, OCC, 256)
            return 0

        lax.fori_loop(0, PAD // 4, expand, 0)

    def round_d(t):
        lo = pick(t, E_FROM)

        def extra(e, _):
            for unit in e_units:
                take(unit, e)
            return 0

        lax.fori_loop(lo, lo + pick(t, E_COUNT), extra, 0)

    leave(d_units)
    leave(e_units)
    lax.fori_loop(0, NCHIP, start_vir, 0)
    gather(d_units, COUNTS_D, compute_d, round_d)

    for i in range(OCC):
        for b in range(4):
            hg[row, 32 * i:32 * i + 32, 128 * b:128 * b + 128] = acc[b, pl.ds(i, 32, stride=OCC), :].astype(BF16)

    leave(h_units)
    for unit in e_units:
        take(unit, NCHIP - 2)
    tables()
    coeff_rows()
    expand_rows()

    def blocks(j):
        select = (iota((512, 256), 0).astype(F32) == targets[pl.ds(j, 1), :]).astype(F32).astype(BF16)
        tiles = dot(hg[j], select)
        lane = iota((32, 128), 1)
        for g in range(2):
            xs = [tiles[32 * i:32 * i + 32, 128 * g:128 * g + 128] for i in range(OCC)]
            sq = jnp.zeros((8, 128), F32)
            for h in range(2):
                ys = []
                for m in range(8 * h, 8 * h + 8):
                    part = None
                    for i in range(OCC):
                        term = xs[i] * cexp[m, j, i:i + 1, 128 * g:128 * g + 128]
                        part = term if i == 0 else part + term
                    block = part.astype(BF16)
                    wide = block.astype(F32)
                    for k in range(4):
                        piece = wide[8 * k:8 * k + 8]
                        sq = sq + piece * piece
                    ys.append(block)
                for bit in (1, 2, 4):
                    low = ((lane >> 4) & bit) == 0
                    zs = list(ys)
                    for i in range(8):
                        if i & bit:
                            continue
                        a, c = ys[i], ys[i | bit]
                        zs[i] = jnp.where(low, a, pltpu.roll(c, PAD * bit, 1))
                        zs[i | bit] = jnp.where(low, pltpu.roll(a, 128 - PAD * bit, 1), c)
                    ys = zs
                for s in range(8):
                    out[j * CAP + 8 * g + s, :, 128 * h:128 * h + 128] = ys[s]
            squares[j, :, 128 * g:128 * g + 128] = sq

    def compute_h(t, q):
        for c in range(2):
            blocks(2 * q + c)

    gather(h_units, COUNTS_H, compute_h, lambda t: None)

    total = jnp.sum(squares[...], axis=1)
    group = (iota((256, 128), 0) >> 4) == iota((256, 128), 1)
    sumout[...] = lax.dot_general(total, group.astype(F32), (((1,), (0,)), ((), ())),
                                  precision=lax.Precision.HIGHEST, preferred_element_type=F32)
    sumbuf[ax] = sumout[...]
    copies = []
    for k in range(1, NX):
        peer = lax.rem(ax + k, NX)
        copy = pltpu.make_async_remote_copy(
            sumout, sumbuf.at[ax], x_send.at[k], x_recv.at[k],
            device_id=(row, peer), device_id_type=pl.DeviceIdType.MESH)
        copy.start()
        copies.append(copy)
    for k in range(UNITS):
        for buf, sem in ((dg, d_send), (hg, h_send)):
            ref = buf.at[pl.ds(0, 31), pl.ds(64 * k, 64)]
            pltpu.make_async_copy(ref, ref, sem.at[k]).wait()
    for buf, sem in ((eo, o_send), (em, m_send)):
        ref = buf.at[pl.ds(0, 31)]
        pltpu.make_async_copy(ref, ref, sem.at[0]).wait()
    for copy in copies:
        copy.wait_recv()
    total_out[...] = (sumbuf[0] + sumbuf[1]) + (sumbuf[2] + sumbuf[3])
    for copy in copies:
        copy.wait_send()


def per_device(density, vir_coeffs, occ_coeffs, shell_len, mu_shell, nu_shell, owner):
    hbm = pl.BlockSpec(memory_space=pl.ANY)
    vmem = pl.BlockSpec(memory_space=pltpu.VMEM)
    dma = pltpu.SemaphoreType.DMA
    blocks, total = pl.pallas_call(
        kernel,
        out_shape=(pltpu.VMEM((512, 32, 256), BF16), pltpu.VMEM((NROW, 128), F32)),
        in_specs=[hbm] * 7,
        out_specs=(vmem, vmem),
        scratch_shapes=[
            pltpu.VMEM((NROW, 256, 512), BF16),
            pltpu.VMEM((NROW, 256, 512), BF16),
            pltpu.VMEM((NCHIP, 512, 1024), BF16),
            pltpu.VMEM((NROW, 8, 512), BF16),
            pltpu.VMEM((NROW, 8, 128), I32),
            pltpu.VMEM((NROW, 64), I32),
            pltpu.VMEM((4, 256, 128), F32),
            pltpu.VMEM((8 * NROW, 8, 128), F32),
            pltpu.VMEM((128, 256), BF16),
            pltpu.VMEM((256, 256), F32),
            pltpu.VMEM((PAD, NROW, OCC, 256), F32),
            pltpu.VMEM((NROW, 256), F32),
            pltpu.VMEM((NROW, 8, 256), F32),
            pltpu.VMEM((NX, NROW, 128), F32),
            pltpu.VMEM((NROW, 128), F32),
            pltpu.VMEM((64, 128), I32),
            pltpu.VMEM((NROW, 128), I32),
            pltpu.SMEM((64, 128), I32),
            pltpu.SMEM((NROW, 128), I32),
            dma((6,)), dma((NCHIP,)), dma((UNITS, NROW)), dma((UNITS, NROW)), dma((NROW,)), dma((NROW,)),
            dma((UNITS,)), dma((UNITS,)), dma((1,)), dma((1,)), dma((NX,)), dma((NX,)), dma((2,)),
        ],
        compiler_params=pltpu.CompilerParams(
            collective_id=0, has_side_effects=True, vmem_limit_bytes=48 * 1024 * 1024),
    )(density.reshape(256, 512), vir_coeffs, occ_coeffs, shell_len,
      mu_shell.reshape(2, 128), nu_shell.reshape(2, 128), owner.reshape(2, 128))
    pair_scale = jnp.sqrt(total[:, :CAP].reshape(512) / (128 * PAD * PAD) + 1e-06)
    return blocks, pair_scale


def solution(mesh):
    return jax.shard_map(
        per_device,
        mesh=mesh,
        in_specs=(
            P("aux", None, "rows"),
            P("rows", None),
            P(None, "rows"),
            P(),
            P("rows"),
            P("rows"),
            P("rows", None),
        ),
        out_specs=(P("rows", "aux", None), P("rows")),
        check_vma=False,
    )
```

time: 91.3 us -> 83.1 us (0.910); the launches traced: 90.1 us -> 83 us
  Pallas kernels: 85.4 us -> 78.3 us
    pallas_call x1, Pallas kernels: 85.4 us -> 78.3 us  [per_device(): pl.pallas_call(kernel, out_shape=(pltpu.VMEM((512, 32, 256), BF16), pltpu...]
where the time goes in v3:
time: 83.1 us; the launch traced here: 83 us
  Pallas kernels  78.3 us (94%)
  local copies, waits for them, and re-layouts  4.06 us (5%)
    pallas_call x1, Pallas kernels, per_device(): pl.pallas_call(kernel, out_shape=(pltpu.VMEM((512, 32, 256), BF16), pltpu...  78.3 us
    unnamed x1, local copies, waits for them, and re-layouts  3.4 us

profile of v3, /device:TPU:24, one launch (start us, length us, event | category | flops | bytes accessed | tf_op | source)
XLA Modules:
  0.0 83.0 jit_solution(13772605815572486571)
XLA Ops:
  0.6 78.3 %shard_map.86 = (bf16[512,32,256]{2,1,0:T(8,128)(2,1)S(1)}, f32[32,128]{1,0:T(8,128)S(1)}) custom-call(bf16[256,512]{1,0:T(8,128)(2,1)} %bitcast.4, bf16[512,16384]{1,0:T(8,128)(2,1)} %vir.1, bf16[8,512]{1,0:T(8,128)(2,1)} %occ.1, s32[32,64]{1,0:T(8,128)} %slen_h.1, s32[2,128]{1,0:T(2,128)} %bitcast.5, s32[2,128]{1,0:T(2,128)} %bitcast.6, s32[2,128]{1,0:T(2,128)} %bitcast.7), custom_call_target="tpu_custom_call" | custom-call | tf_op jit(solution)/shard_map/pallas_call | solution.py:374
  78.9 3.4 %copy.10 = bf16[512,32,256]{2,1,0:T(8,128)(2,1)} copy(bf16[512,32,256]{2,1,0:T(8,128)(2,1)S(1)} %get-tuple-element.6) | data formatting | bytes 16777216
  82.3 0.7 sqrt.7
  (1 shorter events, 0.0 us)

commit v4 on v3

--- a/solution.py
+++ b/solution.py
@@ -259,7 +259,7 @@
                 lined[pl.ds(pl.multiple_of(8 * j, 8), 8), 128 * g:128 * g + 128] = line
             return 0
 
-        lax.fori_loop(0, NROW, coeffs, 0)
+        lax.fori_loop(0, NROW, coeffs, 0, unroll=4)
 
     def expand_rows():
         lined_b = lined[...].astype(BF16)
@@ -267,12 +267,12 @@
         same_slot = (row256 >> 4) == (col256 >> 4)
 
         def expand(n, _):
-            for m in range(4):
-                pick_m = (same_slot & ((row256 & (PAD - 1)) == 4 * n + m)).astype(F32).astype(BF16)
-                cexp[4 * n + m] = dot(lined_b, pick_m).reshape(NROW, OCC, 256)
+            for m in range(8):
+                pick_m = (same_slot & ((row256 & (PAD - 1)) == 8 * n + m)).astype(F32).astype(BF16)
+                cexp[8 * n + m] = dot(lined_b, pick_m).reshape(NROW, OCC, 256)
             return 0
 
-        lax.fori_loop(0, PAD // 4, expand, 0)
+        lax.fori_loop(0, PAD // 8, expand, 0)
 
     def round_d(t):
         lo = pick(t, E_FROM)

time: 83.1 us -> 81.4 us (0.980)
  Pallas kernels: 78.3 us -> 76.6 us
    pallas_call x1, Pallas kernels: 78.3 us -> 76.6 us  [per_device(): pl.pallas_call(kernel, out_shape=(pltpu.VMEM((512, 32, 256), BF16), pltpu...]
where the time goes in v4:
time: 81.4 us; the launch traced here: 81.3 us
  Pallas kernels  76.6 us (94%)
  local copies, waits for them, and re-layouts  4.06 us (5%)
    pallas_call x1, Pallas kernels, per_device(): pl.pallas_call(kernel, out_shape=(pltpu.VMEM((512, 32, 256), BF16), pltpu...  76.6 us
    unnamed x1, local copies, waits for them, and re-layouts  3.4 us

profile of v4, /device:TPU:24, one launch (start us, length us, event | category | flops | bytes accessed | tf_op | source)
XLA Modules:
  0.0 81.3 jit_solution(12294946172807025028)
XLA Ops:
  0.6 76.6 %shard_map.86 = (bf16[512,32,256]{2,1,0:T(8,128)(2,1)S(1)}, f32[32,128]{1,0:T(8,128)S(1)}) custom-call(bf16[256,512]{1,0:T(8,128)(2,1)} %bitcast.4, bf16[512,16384]{1,0:T(8,128)(2,1)} %vir.1, bf16[8,512]{1,0:T(8,128)(2,1)} %occ.1, s32[32,64]{1,0:T(8,128)} %slen_h.1, s32[2,128]{1,0:T(2,128)} %bitcast.5, s32[2,128]{1,0:T(2,128)} %bitcast.6, s32[2,128]{1,0:T(2,128)} %bitcast.7), custom_call_target="tpu_custom_call" | custom-call | tf_op jit(solution)/shard_map/pallas_call | solution.py:374
  77.2 3.4 %copy.10 = bf16[512,32,256]{2,1,0:T(8,128)(2,1)} copy(bf16[512,32,256]{2,1,0:T(8,128)(2,1)S(1)} %get-tuple-element.6) | data formatting | bytes 16777216
  80.6 0.7 sqrt.7
  (1 shorter events, 0.0 us)

commit v5 on v4

--- a/solution.py
+++ b/solution.py
@@ -315,9 +315,8 @@
                         term = xs[i] * cexp[m, j, i:i + 1, 128 * g:128 * g + 128]
                         part = term if i == 0 else part + term
                     block = part.astype(BF16)
-                    wide = block.astype(F32)
                     for k in range(4):
-                        piece = wide[8 * k:8 * k + 8]
+                        piece = part[8 * k:8 * k + 8]
                         sq = sq + piece * piece
                     ys.append(block)
                 for bit in (1, 2, 4):

time: 81.4 us -> 81.2 us (level)
  no operation moved by 1% of the time
where the time goes in v5:
time: 81.2 us; the launch traced here: 81.1 us
  Pallas kernels  76.3 us (94%)
  local copies, waits for them, and re-layouts  4.06 us (5%)
    pallas_call x1, Pallas kernels, per_device(): pl.pallas_call(kernel, out_shape=(pltpu.VMEM((512, 32, 256), BF16), pltpu...  76.3 us
    unnamed x1, local copies, waits for them, and re-layouts  3.4 us

profile of v5, /device:TPU:24, one launch (start us, length us, event | category | flops | bytes accessed | tf_op | source)
XLA Modules:
  0.0 81.1 jit_solution(9983777661293880721)
XLA Ops:
  0.6 76.3 %shard_map.86 = (bf16[512,32,256]{2,1,0:T(8,128)(2,1)S(1)}, f32[32,128]{1,0:T(8,128)S(1)}) custom-call(bf16[256,512]{1,0:T(8,128)(2,1)} %bitcast.4, bf16[512,16384]{1,0:T(8,128)(2,1)} %vir.1, bf16[8,512]{1,0:T(8,128)(2,1)} %occ.1, s32[32,64]{1,0:T(8,128)} %slen_h.1, s32[2,128]{1,0:T(2,128)} %bitcast.5, s32[2,128]{1,0:T(2,128)} %bitcast.6, s32[2,128]{1,0:T(2,128)} %bitcast.7), custom_call_target="tpu_custom_call" | custom-call | tf_op jit(solution)/shard_map/pallas_call | solution.py:373
  77.0 3.4 %copy.10 = bf16[512,32,256]{2,1,0:T(8,128)(2,1)} copy(bf16[512,32,256]{2,1,0:T(8,128)(2,1)S(1)} %get-tuple-element.6) | data formatting | bytes 16777216
  80.4 0.7 sqrt.7
  (1 shorter events, 0.0 us)
